TPU v7x, 128 devices: a whole 4x4x4 slice. The times are simulated.
128 devices in a mesh: ctx: 32 (over z, x, core), head: 4 (over y).
Axes of the slice: x: 4, y: 4, z: 4, core: 2. Of those that a mesh axis runs over, the one named last changes fastest.
Arguments:
- queries: bfloat16 [16384, 4096], P('ctx', 'head'), may hold values from -8 to 8
- keys: bfloat16 [16384, 512], P('ctx', 'head'), may hold values from -8 to 8
- values: bfloat16 [16384, 512], P('ctx', 'head'), may hold values from -6 to 6
- distances: int32 [4, 3], P('head'), may hold values from 1 to 31, as said below
- out_weight: bfloat16 [4096, 2048], P('head'), may hold values from -0.09375 to 0.09375
- residual: bfloat16 [16384, 2048], P(('ctx', 'head')), may hold values from -6 to 6
- norm_gain: float32 [2048], replicated, may hold values from 0.25 to 1.75
- expert_gate_up: bfloat16 [128, 2048, 1536], P(('ctx', 'head')), may hold values from -0.125 to 0.125
- expert_down: bfloat16 [128, 768, 2048], P(('ctx', 'head')), may hold values from -0.21875 to 0.21875
- routes: int32 [16384, 8], P(('ctx', 'head')), may hold values from 0 to 127, all different within a row; in each aligned block of 128 rows (0 to 127, 128 to 255, ...) at most 16 rows name the same one
- route_weights: float32 [16384, 8], P(('ctx', 'head')), may hold values from 0.05 to 0.5
Outputs:
- attended: bfloat16 [16384, 2048], P(('ctx', 'head'))
- moe_out: bfloat16 [16384, 2048], P(('ctx', 'head'))
Inputs may be any that keep to these rules, and one draw needn't show every extreme that they name: Each row holds 3 different distances; some row holds the distance 16384 // 1024. `routes`: among the 128 rows of one device, no expert is named by more than 16 rows.
All inputs are finite; a program needn't handle non-finite values.
Results may differ from a plain program's by a relative error of at most 0.01.
Values may be sent and summed in bfloat16 or wider, within the bound.
No kernel may reach another device: no remote copies, remote signals or barrier semaphores. Data moves between devices by JAX's collectives and lax.ppermute only.
A program may use at most 128 MiB of HBM per device.

v0:
```python
import functools
import math

import jax
import jax.numpy as jnp
from jax import lax
from jax.experimental import pallas as pl
from jax.experimental.pallas import tpu as pltpu
from jax.sharding import PartitionSpec as P

HD = 128
FFE = 768
TOP = 8
BLK = 128
DIST = 3
CAP = 16
CHUNKS = (8, 8)
ALL = ("ctx", "head")
BF16 = jnp.bfloat16
F32 = jnp.float32
NT = (((1,), (1,)), ((), ()))
TN = (((0,), (0,)), ((), ()))
EXPONENT = math.log2(math.e) / math.sqrt(HD)


def params(steps=1, limit=56):
    return pltpu.CompilerParams(
        dimension_semantics=("arbitrary",) * steps, vmem_limit_bytes=limit * 1024 * 1024
    )


def held(array):
    return pltpu.with_memory_space_constraint(array, pltpu.VMEM)


def attention_kernel(
    first, stride, place, wanted, q_ref, k_ref, v_ref, far0_ref, far1_ref, far2_ref, weight_ref, *refs
):
    out_refs, (mixed_ref, w_ref, sem) = refs[:-3], refs[-3:]
    step = pl.program_id(0)
    load = pltpu.make_async_copy(weight_ref, w_ref, sem)
    pl.when(step == 0)(load.start)
    steps = len(out_refs)
    blocks = k_ref.shape[0] // BLK
    heads = q_ref.shape[1] // HD
    block = lax.rem(place[1] + first + stride * step, blocks)
    far_refs = (far0_ref, far1_ref, far2_ref)

    def attend(wide):
        rows = lax.broadcasted_iota(jnp.int32, (2 * BLK, BLK), 0)
        columns = lax.broadcasted_iota(jnp.int32, (2 * BLK, BLK), 1)
        bias = jnp.where(rows > columns + lax.rem(block, 2) * BLK, -jnp.inf, 0.0)
        bias = jnp.concatenate([bias] * heads, axis=1)
        reach = [jnp.where(place[0] >= wanted[0, j], 0.0, -jnp.inf) for j in range(DIST)]
        keys = jnp.concatenate([k_ref[:wide]] + [r[0] for r in far_refs], axis=0)
        values = jnp.concatenate([v_ref[:wide]] + [r[1] for r in far_refs], axis=0)
        query = jnp.concatenate([q_ref[:, n * HD : (n + 1) * HD] for n in range(heads)], axis=0)
        score = lax.dot_general(keys, query, NT, preferred_element_type=F32)
        early = wide - 2 * BLK
        parts = [score[:early]] if early else []
        parts.append(score[early:wide] + bias)
        for j in range(DIST):
            parts.append(score[wide + j * BLK : wide + (j + 1) * BLK] + reach[j])
        score = jnp.concatenate(parts, axis=0)
        highest = jnp.max(score, axis=0, keepdims=True)
        weight = jnp.exp2((score - highest) * EXPONENT)
        denominator = jnp.sum(weight, axis=0, keepdims=True)
        mixed = lax.dot_general(values, weight.astype(BF16), TN, preferred_element_type=F32)
        mixed = mixed / denominator
        for n in range(heads):
            mixed_ref[pl.ds(step * BLK, BLK), n * HD : (n + 1) * HD] = (
                mixed[:, n * BLK : (n + 1) * BLK].T.astype(BF16)
            )

    for pair in range(blocks // 2):
        pl.when(block // 2 == pair)(functools.partial(attend, 2 * BLK * (pair + 1)))

    @pl.when(step == steps - 1)
    def _():
        load.wait()
        for i, out_ref in enumerate(out_refs):
            out_ref[...] = jnp.dot(
                mixed_ref[i * BLK : (i + 1) * BLK], w_ref[...], preferred_element_type=F32
            ).astype(BF16)


def attention(place, wanted, queries, keys, values, far, out_weight, first, stride, steps):
    length, wide = queries.shape
    width = out_weight.shape[1]
    at = lambda i, place: lax.rem(place[1] + first + stride * i, length // BLK)
    whole = lambda shape: pl.BlockSpec(
        shape, lambda i, p, w: (0,) * len(shape), pipeline_mode=pl.Buffered(1)
    )
    return pl.pallas_call(
        functools.partial(attention_kernel, first, stride),
        grid_spec=pltpu.PrefetchScalarGridSpec(
            num_scalar_prefetch=2,
            grid=(steps,),
            in_specs=[
                pl.BlockSpec((BLK, wide), lambda i, p, w: (at(i, p), 0)),
                whole(keys.shape),
                whole(values.shape),
            ]
            + [pl.BlockSpec((2, BLK, HD), lambda i, p, w: (0, at(i, p), 0))] * DIST
            + [pl.BlockSpec(memory_space=pl.ANY)],
            out_specs=(whole((BLK, width)),) * steps,
            scratch_shapes=[
                pltpu.VMEM((steps * BLK, wide), BF16),
                pltpu.VMEM(out_weight.shape, BF16),
                pltpu.SemaphoreType.DMA,
            ],
        ),
        out_shape=(jax.ShapeDtypeStruct((BLK, width), BF16),) * steps,
        compiler_params=params(),
        name="attention",
    )(place, wanted, queries, keys, values, *far, out_weight)


def tables_kernel(routes_ref, weights_ref, *refs):
    top, tokens = routes_ref.shape
    chunks = len(CHUNKS)
    send_refs, table_refs, spread_refs = refs[:chunks], refs[chunks : -chunks], refs[-chunks:]
    experts = spread_refs[0].shape[0]
    names = lax.broadcasted_iota(jnp.int32, (experts, tokens), 0)
    chosen = jnp.zeros((experts, tokens), F32)
    weight = jnp.zeros((experts, tokens), F32)
    for k in range(top):
        here = routes_ref[k : k + 1, :] == names
        chosen = jnp.where(here, 1.0, chosen)
        weight = jnp.where(here, weights_ref[k : k + 1, :], weight)
    before = (
        lax.broadcasted_iota(jnp.int32, (tokens, tokens), 0)
        < lax.broadcasted_iota(jnp.int32, (tokens, tokens), 1)
    ).astype(BF16)
    place = jnp.dot(chosen.astype(BF16), before, preferred_element_type=F32)
    place = jnp.where(chosen > 0.0, place, -1.0)
    high = weight.astype(BF16).astype(F32)
    low = weight - high

    first = 0
    for send_ref, table_ref, spread_ref, slots in zip(
        send_refs, table_refs, spread_refs, CHUNKS
    ):

        def spread(value):
            for s in range(slots):
                spread_ref[:, s, :] = jnp.where(place == float(first + s), value, 0.0)
            return spread_ref[...].reshape(experts * slots, tokens).astype(BF16)

        send_ref[...] = spread(1.0)
        table_ref[:, :tokens] = spread(high)
        table_ref[:, tokens:] = spread(low)
        first += slots


def tables(routes, route_weights, experts):
    tokens = routes.shape[0]
    shapes = lambda columns: tuple(
        jax.ShapeDtypeStruct((experts * slots, columns), BF16) for slots in CHUNKS
    )
    made = pl.pallas_call(
        tables_kernel,
        out_shape=shapes(tokens) + shapes(2 * tokens),
        scratch_shapes=[pltpu.VMEM((experts, slots, tokens), F32) for slots in CHUNKS],
        compiler_params=params(0),
        name="tables",
    )(routes.T, route_weights.T)
    return made[: len(CHUNKS)], made[len(CHUNKS) :]


def norm_kernel(
    own_ref, r1_ref, r2_ref, r3_ref, residual_ref, gain_ref, send_ref, attended_ref, normed_ref, out_ref
):
    @pl.when(pl.program_id(0) == 0)
    def _():
        total = residual_ref[...].astype(F32) + own_ref[...].astype(F32)
        for part_ref in (r1_ref, r2_ref, r3_ref):
            total = total + part_ref[...].astype(F32)
        attended = total.astype(BF16)
        attended_ref[...] = attended
        wide = attended.astype(F32)
        inverse = lax.rsqrt(jnp.mean(wide * wide, axis=1, keepdims=True) + 1e-06)
        normed_ref[...] = (wide * inverse * gain_ref[...]).astype(BF16)

    out_ref[...] = jnp.dot(send_ref[...], normed_ref[...], preferred_element_type=F32).astype(BF16)


def norm_dispatch(own, others, residual, gain, send):
    tokens, width = residual.shape
    rows = send.shape[0]
    step = 512
    whole = lambda shape: pl.BlockSpec(shape, lambda i: (0,) * len(shape))
    return pl.pallas_call(
        norm_kernel,
        grid=(rows // step,),
        in_specs=[whole((tokens, width))]
        + [pl.BlockSpec(memory_space=pltpu.VMEM)] * 3
        + [whole((tokens, width)), whole((1, width)), pl.BlockSpec((step, tokens), lambda i: (i, 0))],
        out_specs=(
            whole((tokens, width)),
            whole((tokens, width)),
            pl.BlockSpec((step, width), lambda i: (i, 0)),
        ),
        out_shape=(
            jax.ShapeDtypeStruct((tokens, width), BF16),
            jax.ShapeDtypeStruct((tokens, width), BF16),
            jax.ShapeDtypeStruct((rows, width), BF16),
        ),
        compiler_params=params(),
        name="norm_dispatch",
    )(own, *others, residual, gain.reshape(1, width), send)


def dispatch_kernel(send_ref, normed_ref, out_ref):
    out_ref[...] = jnp.dot(send_ref[...], normed_ref[...], preferred_element_type=F32).astype(BF16)


def dispatch(send, normed):
    tokens, width = normed.shape
    rows = send.shape[0]
    step = 512
    return pl.pallas_call(
        dispatch_kernel,
        grid=(rows // step,),
        in_specs=[
            pl.BlockSpec((step, tokens), lambda i: (i, 0)),
            pl.BlockSpec((tokens, width), lambda i: (0, 0)),
        ],
        out_specs=pl.BlockSpec((step, width), lambda i: (i, 0)),
        out_shape=jax.ShapeDtypeStruct((rows, width), BF16),
        compiler_params=params(),
        name="dispatch",
    )(send, normed)


def expert_kernel(x_ref, gate_up_ref, down_ref, out_ref):
    projected = jnp.dot(x_ref[...], gate_up_ref[0], preferred_element_type=F32)
    gate, up = projected[:, :FFE], projected[:, FFE:]
    hidden = (gate / (1.0 + jnp.exp(-gate)) * up).astype(BF16)
    out_ref[...] = jnp.dot(hidden, down_ref[0], preferred_element_type=F32).astype(BF16)


def expert(x, gate_up, down):
    rows, width = x.shape
    step = 256
    whole = lambda shape: pl.BlockSpec(
        shape, lambda i: (0,) * len(shape), pipeline_mode=pl.Buffered(1)
    )
    return pl.pallas_call(
        expert_kernel,
        grid=(rows // step,),
        in_specs=[
            pl.BlockSpec((step, width), lambda i: (i, 0)),
            whole(gate_up.shape),
            whole(down.shape),
        ],
        out_specs=pl.BlockSpec((step, width), lambda i: (i, 0)),
        out_shape=jax.ShapeDtypeStruct((rows, width), BF16),
        compiler_params=params(),
        name="expert",
    )(x, gate_up, down)


def combine_kernel(table_ref, rows_ref, *refs):
    before_ref, (out_ref, total_ref) = (refs[0] if len(refs) == 3 else None), refs[-2:]
    step = pl.program_id(0)
    tokens = out_ref.shape[0]
    part = lax.dot_general(table_ref[...], rows_ref[...], TN, preferred_element_type=F32)
    part = part[:tokens] + part[tokens:]

    @pl.when(step == 0)
    def _():
        total_ref[...] = part if before_ref is None else part + before_ref[...]

    @pl.when(step > 0)
    def _():
        total_ref[...] += part

    @pl.when(step == pl.num_programs(0) - 1)
    def _():
        out_ref[...] = total_ref[...].astype(out_ref.dtype)


def combine(table, rows, before, dtype):
    count, width = rows.shape
    tokens = table.shape[1] // 2
    step = 512
    whole = lambda shape: pl.BlockSpec(shape, lambda i: (0,) * len(shape))
    operands = (table, rows) + (() if before is None else (before,))
    return pl.pallas_call(
        combine_kernel,
        grid=(count // step,),
        in_specs=[
            pl.BlockSpec((step, 2 * tokens), lambda i: (i, 0)),
            pl.BlockSpec((step, width), lambda i: (i, 0)),
        ]
        + ([] if before is None else [whole(before.shape)]),
        out_specs=whole((tokens, width)),
        out_shape=jax.ShapeDtypeStruct((tokens, width), dtype),
        scratch_shapes=[pltpu.VMEM((tokens, width), F32)],
        compiler_params=params(),
        name="combine",
    )(*operands)


def fetch(packed, distance):
    shards = lax.axis_size("ctx")

    def back(by, block):
        return lax.ppermute(block, "ctx", [(i, i + by) for i in range(shards - by)])

    return lax.switch(
        distance,
        [lambda block: block] + [functools.partial(back, by) for by in range(1, shards)],
        packed,
    )


def body(
    queries,
    keys,
    values,
    distances,
    out_weight,
    residual,
    norm_gain,
    expert_gate_up,
    expert_down,
    routes,
    route_weights,
):
    tokens, width = residual.shape
    devices = lax.axis_size(ALL)
    me, head = lax.axis_index("ctx"), lax.axis_index("head")
    packed = jnp.stack([keys, values])
    far = [fetch(packed, distances[0, j]) for j in range(DIST)]
    send, table = tables(routes, route_weights, devices)
    group = lax.axis_size("head")

    place = jnp.stack([me, head])

    def project(place, first, stride, steps):
        return attention(
            place, distances, queries, keys, values, far, out_weight, first, stride, steps
        )

    def hand(block, by):
        return lax.ppermute(block, "head", [(i, (i + by) % group) for i in range(group)])

    (two,) = project(place, 2, 1, 1)
    two, place = lax.optimization_barrier((two, place))
    two = hand(two, 2)
    one, three = project(place, 1, 2, 2)
    one, three, place = lax.optimization_barrier((one, three, place))
    others = [held(a) for a in (two, hand(one, 1), hand(three, 3))]
    (own,) = project(place, 0, 1, 1)
    attended, normed, first = norm_dispatch(own, others, residual, norm_gain, send[0])
    exchange = lambda a: lax.all_to_all(a, ALL, split_axis=0, concat_axis=0, tiled=True)
    arrived = [exchange(first)] + [exchange(dispatch(s, normed)) for s in send[1:]]
    returned = [exchange(expert(a, expert_gate_up, expert_down)) for a in arrived]
    total = None
    for c, (t, r) in enumerate(zip(table, returned)):
        total = combine(t, r, total, BF16 if c == len(CHUNKS) - 1 else F32)
    return (attended, total)


def solution(mesh):
    return jax.shard_map(
        body,
        mesh=mesh,
        in_specs=(
            P("ctx", "head"),
            P("ctx", "head"),
            P("ctx", "head"),
            P("head", None),
            P("head", None),
            P(ALL, None),
            P(),
            P(ALL, None, None),
            P(ALL, None, None),
            P(ALL, None),
            P(ALL, None),
        ),
        out_specs=(P(ALL, None), P(ALL, None)),
        check_vma=False,
    )
```

profile of v0, /device:TPU:1, one launch (start us, length us, event | category | flops | bytes accessed | tf_op | source)
XLA Modules:
  0.0 316.8 jit_solution(9067311625801396541)
XLA Ops:
  0.6 1.4 fusion
  4.0 1.0 pad_maximum_fusion
  5.0 11.2 %conditional.5 = (bf16[2,512,128]{2,1,0:T(8,128)(2,1)}) conditional(s32[]{:T(128)} %bitcast.6, bf16[2,512,128]{2,1,0:T(8,128)(2,1)S(1)} %pad_maximum_fusion, bf16[2,512,128]{2,1,0:T(8,128)(2,1)S(1)} %pad_maximum_fusion, bf16[2,512,128]{2,1,0:T(8,128)(2,1)S(1)} %pad_maximum_fusion, ...), branch_computations={%region_64.0_spmd, %region_65.0_spmd, %region_66.0_spmd, %region_6... | conditional | bytes 1048624 | solution.py:312
  5.1 8.5 %collective-permute-start.78 = (bf16[2,512,128]{2,1,0:T(8,128)(2,1)S(1)}, bf16[2,512,128]{2,1,0:T(8,128)(2,1)}, u32[]{:S(2)}, u32[]{:S(2)}) collective-permute-start(bf16[2,512,128]{2,1,0:T(8,128)(2,1)S(1)} %param.81), channel_id=1, source_target_pairs={{0,68},{4,72},{8,76},{12,80},{16,84},{20,88},{24,92},{28,96},{32,1... | collective-permute-start | bytes 786440 | tf_op jit(solution)/shard_map/cond/branch_17_fun/ppermute | solution.py:310
  13.6 2.6 collective-permute-done.78
  16.2 14.3 %conditional.4 = (bf16[2,512,128]{2,1,0:T(8,128)(2,1)}) conditional(s32[]{:T(128)} %bitcast.5, bf16[2,512,128]{2,1,0:T(8,128)(2,1)S(1)} %pad_maximum_fusion, bf16[2,512,128]{2,1,0:T(8,128)(2,1)S(1)} %pad_maximum_fusion, bf16[2,512,128]{2,1,0:T(8,128)(2,1)S(1)} %pad_maximum_fusion, ...), branch_computations={%region_32.0_spmd, %region_33.0_spmd, %region_34.0_spmd, %region_3... | conditional | bytes 1048624 | solution.py:312
  16.2 9.2 %collective-permute-start.49 = (bf16[2,512,128]{2,1,0:T(8,128)(2,1)S(1)}, bf16[2,512,128]{2,1,0:T(8,128)(2,1)}, u32[]{:S(2)}, u32[]{:S(2)}) collective-permute-start(bf16[2,512,128]{2,1,0:T(8,128)(2,1)S(1)} %param.51), channel_id=1, source_target_pairs={{0,76},{4,80},{8,84},{12,88},{16,92},{20,96},{24,100},{28,104},{32... | collective-permute-start | bytes 786440 | tf_op jit(solution)/shard_map/cond/branch_19_fun/ppermute | solution.py:310
  25.4 5.1 %collective-permute-done.49 = bf16[2,512,128]{2,1,0:T(8,128)(2,1)} collective-permute-done((bf16[2,512,128]{2,1,0:T(8,128)(2,1)S(1)}, bf16[2,512,128]{2,1,0:T(8,128)(2,1)}, u32[]{:S(2)}, u32[]{:S(2)}) %collective-permute-start.49) | collective-permute-done | bytes 262176 | tf_op jit(solution)/shard_map/cond/branch_19_fun/ppermute | solution.py:310
  30.5 6.4 %conditional.3 = (bf16[2,512,128]{2,1,0:T(8,128)(2,1)}) conditional(s32[]{:T(128)} %bitcast.2, bf16[2,512,128]{2,1,0:T(8,128)(2,1)S(1)} %pad_maximum_fusion, bf16[2,512,128]{2,1,0:T(8,128)(2,1)S(1)} %pad_maximum_fusion, bf16[2,512,128]{2,1,0:T(8,128)(2,1)S(1)} %pad_maximum_fusion, ...), branch_computations={%region_0.0_spmd, %region_1.0_spmd, %region_2.0_spmd, %region_3.0_... | conditional | bytes 1048624 | solution.py:312
  30.5 2.0 collective-permute-start.4
  32.5 4.4 %collective-permute-done.4 = bf16[2,512,128]{2,1,0:T(8,128)(2,1)} collective-permute-done((bf16[2,512,128]{2,1,0:T(8,128)(2,1)S(1)}, bf16[2,512,128]{2,1,0:T(8,128)(2,1)}, u32[]{:S(2)}, u32[]{:S(2)}) %collective-permute-start.4) | collective-permute-done | bytes 262176 | tf_op jit(solution)/shard_map/cond/branch_5_fun/ppermute | solution.py:310
  37.6 5.5 %attention.3 = bf16[128,2048]{1,0:T(8,128)(2,1)} custom-call(s32[2]{0:T(128)} %pad_add_fusion.place, s32[1,3]{1,0:T(1,128)} %wanted.5, bf16[512,1024]{1,0:T(8,128)(2,1)} %q_ref.5, bf16[512,128]{1,0:T(8,128)(2,1)} %k_ref.5, bf16[512,128]{1,0:T(8,128)(2,1)} %v_ref.5, bf16[2,512,128]{2,1,0:T(8,128)(2,1)} %get-tuple-element.228.far0_ref, ...), custom_call_target="tpu_custom_call" | custom-call | tf_op jit(solution)/shard_map/attention/pallas_call | solution.py:94
  43.3 7.1 %attention.4 = (bf16[128,2048]{1,0:T(8,128)(2,1)}, bf16[128,2048]{1,0:T(8,128)(2,1)}) custom-call(s32[2]{0:T(128)} %pad_add_fusion.place, s32[1,3]{1,0:T(1,128)} %wanted.5, bf16[512,1024]{1,0:T(8,128)(2,1)} %q_ref.5, bf16[512,128]{1,0:T(8,128)(2,1)} %k_ref.5, bf16[512,128]{1,0:T(8,128)(2,1)} %v_ref.5, bf16[2,512,128]{2,1,0:T(8,128)(2,1)} %get-tuple-element.228.far0_ref, ...), custom_call_target="tpu_custom_call" | custom-call | tf_op jit(solution)/shard_map/attention/pallas_call | solution.py:94
  50.4 2.0 collective-permute-start.94
  52.4 2.5 collective-permute-start.95
  54.8 5.5 %attention.5.own_ref = bf16[128,2048]{1,0:T(8,128)(2,1)} custom-call(s32[2]{0:T(128)} %pad_add_fusion.place, s32[1,3]{1,0:T(1,128)} %wanted.5, bf16[512,1024]{1,0:T(8,128)(2,1)} %q_ref.5, bf16[512,128]{1,0:T(8,128)(2,1)} %k_ref.5, bf16[512,128]{1,0:T(8,128)(2,1)} %v_ref.5, bf16[2,512,128]{2,1,0:T(8,128)(2,1)} %get-tuple-element.228.far0_ref, ...), custom_call_target="tpu_custom_call" | custom-call | tf_op jit(solution)/shard_map/attention/pallas_call | solution.py:94
  60.3 3.8 %tables.1 = (bf16[1024,128]{1,0:T(8,128)(2,1)}, bf16[1024,128]{1,0:T(8,128)(2,1)}, bf16[1024,256]{1,0:T(8,128)(2,1)}, bf16[1024,256]{1,0:T(8,128)(2,1)}) custom-call(s32[8,128]{1,0:T(8,128)} %bitcast.25, f32[8,128]{1,0:T(8,128)} %bitcast.26), custom_call_target="tpu_custom_call" | custom-call | tf_op jit(solution)/shard_map/tables/pallas_call | solution.py:161
  64.1 4.9 %collective-permute-done.94.r2_ref = bf16[128,2048]{1,0:T(8,128)(2,1)S(1)} collective-permute-done((bf16[128,2048]{1,0:T(8,128)(2,1)}, bf16[128,2048]{1,0:T(8,128)(2,1)S(1)}, u32[]{:S(2)}, u32[]{:S(2)}) %collective-permute-start.94) | collective-permute-done | bytes 524320 | tf_op jit(solution)/shard_map/ppermute | solution.py:348
  69.1 4.9 %norm_dispatch.1 = (bf16[128,2048]{1,0:T(8,128)(2,1)}, bf16[128,2048]{1,0:T(8,128)(2,1)}, bf16[1024,2048]{1,0:T(8,128)(2,1)}) custom-call(bf16[128,2048]{1,0:T(8,128)(2,1)} %attention.5.own_ref, bf16[128,2048]{1,0:T(8,128)(2,1)S(1)} %collective-permute-done.93.r1_ref, bf16[128,2048]{1,0:T(8,128)(2,1)S(1)} %collective-permute-done.94.r2_ref, ...), custom_call_target="tpu_custom_call" | custom-call | tf_op jit(solution)/shard_map/norm_dispatch/pallas_call | solution.py:193
  74.0 13.4 %all-to-all-start.2 = ((bf16[128,8,2048]{2,1,0:T(8,128)(2,1)}), bf16[128,8,2048]{2,1,0:T(8,128)(2,1)}, u32[]{:S(2)}, u32[]{:S(2)}) async-start(bf16[128,8,2048]{2,1,0:T(8,128)(2,1)} %bitcast.21), calls=%async_computation.2 | async-start | bytes 8388608 | tf_op jit(solution)/shard_map/all_to_all | solution.py:358
  87.4 3.9 %dispatch.1 = bf16[1024,2048]{1,0:T(8,128)(2,1)} custom-call(bf16[1024,128]{1,0:T(8,128)(2,1)} %get-tuple-element.221.send_ref, bf16[128,2048]{1,0:T(8,128)(2,1)} %get-tuple-element.222.normed_ref), custom_call_target="tpu_custom_call" | custom-call | tf_op jit(solution)/shard_map/dispatch/pallas_call | solution.py:222
  91.4 48.9 %all-to-all-done.2 = bf16[128,8,2048]{2,1,0:T(8,128)(2,1)} async-done(((bf16[128,8,2048]{2,1,0:T(8,128)(2,1)}), bf16[128,8,2048]{2,1,0:T(8,128)(2,1)}, u32[]{:S(2)}, u32[]{:S(2)}) %all-to-all-start.2) | async-done | bytes 4194336 | tf_op jit(solution)/shard_map/all_to_all | solution.py:358
  140.3 4.8 %all-to-all-start = ((bf16[128,8,2048]{2,1,0:T(8,128)(2,1)}), bf16[128,8,2048]{2,1,0:T(8,128)(2,1)}, u32[]{:S(2)}, u32[]{:S(2)}) async-start(bf16[128,8,2048]{2,1,0:T(8,128)(2,1)} %bitcast.20), calls=%async_computation | async-start | bytes 8388608 | tf_op jit(solution)/shard_map/all_to_all | solution.py:358
  145.1 15.6 %expert.3 = bf16[1024,2048]{1,0:T(8,128)(2,1)} custom-call(bf16[1024,2048]{1,0:T(8,128)(2,1)} %bitcast.15.x_ref, bf16[1,2048,1536]{2,1,0:T(8,128)(2,1)} %gate_up_ref.3, bf16[1,768,2048]{2,1,0:T(8,128)(2,1)} %down_ref.3), custom_call_target="tpu_custom_call" | custom-call | tf_op jit(solution)/shard_map/expert/pallas_call | solution.py:249
  160.6 37.0 %all-to-all-done = bf16[128,8,2048]{2,1,0:T(8,128)(2,1)} async-done(((bf16[128,8,2048]{2,1,0:T(8,128)(2,1)}), bf16[128,8,2048]{2,1,0:T(8,128)(2,1)}, u32[]{:S(2)}, u32[]{:S(2)}) %all-to-all-start) | async-done | bytes 4194336 | tf_op jit(solution)/shard_map/all_to_all | solution.py:358
  197.6 4.8 %all-to-all-start.3 = ((bf16[128,8,2048]{2,1,0:T(8,128)(2,1)}), bf16[128,8,2048]{2,1,0:T(8,128)(2,1)}, u32[]{:S(2)}, u32[]{:S(2)}) async-start(bf16[128,8,2048]{2,1,0:T(8,128)(2,1)} %bitcast.19), calls=%async_computation.3 | async-start | bytes 8388608 | tf_op jit(solution)/shard_map/all_to_all | solution.py:358
  202.4 15.5 %expert.2 = bf16[1024,2048]{1,0:T(8,128)(2,1)} custom-call(bf16[1024,2048]{1,0:T(8,128)(2,1)} %bitcast.11.x_ref, bf16[1,2048,1536]{2,1,0:T(8,128)(2,1)} %gate_up_ref.3, bf16[1,768,2048]{2,1,0:T(8,128)(2,1)} %down_ref.3), custom_call_target="tpu_custom_call" | custom-call | tf_op jit(solution)/shard_map/expert/pallas_call | solution.py:249
  217.9 37.1 %all-to-all-done.3 = bf16[128,8,2048]{2,1,0:T(8,128)(2,1)} async-done(((bf16[128,8,2048]{2,1,0:T(8,128)(2,1)}), bf16[128,8,2048]{2,1,0:T(8,128)(2,1)}, u32[]{:S(2)}, u32[]{:S(2)}) %all-to-all-start.3) | async-done | bytes 4194336 | tf_op jit(solution)/shard_map/all_to_all | solution.py:358
  255.0 4.8 %all-to-all-start.1 = ((bf16[128,8,2048]{2,1,0:T(8,128)(2,1)}), bf16[128,8,2048]{2,1,0:T(8,128)(2,1)}, u32[]{:S(2)}, u32[]{:S(2)}) async-start(bf16[128,8,2048]{2,1,0:T(8,128)(2,1)} %bitcast.18), calls=%async_computation.1 | async-start | bytes 8388608 | tf_op jit(solution)/shard_map/all_to_all | solution.py:358
  259.8 4.4 %combine.2.refs_0_ = f32[128,2048]{1,0:T(8,128)} custom-call(bf16[1024,256]{1,0:T(8,128)(2,1)} %get-tuple-element.223.table_ref, bf16[1024,2048]{1,0:T(8,128)(2,1)} %bitcast.17.rows_ref), custom_call_target="tpu_custom_call" | custom-call | tf_op jit(solution)/shard_map/combine/pallas_call | solution.py:290
  264.1 48.2 %all-to-all-done.1 = bf16[128,8,2048]{2,1,0:T(8,128)(2,1)} async-done(((bf16[128,8,2048]{2,1,0:T(8,128)(2,1)}), bf16[128,8,2048]{2,1,0:T(8,128)(2,1)}, u32[]{:S(2)}, u32[]{:S(2)}) %all-to-all-start.1) | async-done | bytes 4194336 | tf_op jit(solution)/shard_map/all_to_all | solution.py:358
  312.3 4.5 %combine.3 = bf16[128,2048]{1,0:T(8,128)(2,1)} custom-call(bf16[1024,256]{1,0:T(8,128)(2,1)} %get-tuple-element.220.table_ref, bf16[1024,2048]{1,0:T(8,128)(2,1)} %bitcast.13.rows_ref, f32[128,2048]{1,0:T(8,128)} %combine.2.refs_0_), custom_call_target="tpu_custom_call" | custom-call | tf_op jit(solution)/shard_map/combine/pallas_call | solution.py:290
  (4 shorter events, 0.9 us)
Async XLA Ops:
  5.1 11.2 %collective-permute-start.78 = (bf16[2,512,128]{2,1,0:T(8,128)(2,1)S(1)}, bf16[2,512,128]{2,1,0:T(8,128)(2,1)}, u32[]{:S(2)}, u32[]{:S(2)}) collective-permute-start(bf16[2,512,128]{2,1,0:T(8,128)(2,1)S(1)} %param.81), channel_id=1, source_target_pairs={{0,68},{4,72},{8,76},{12,80},{16,84},{20,88},{24,92},{28,96},{32,1... | collective-permute-start | bytes 786440 | tf_op jit(solution)/shard_map/cond/branch_17_fun/ppermute | solution.py:310
  16.2 14.3 %collective-permute-start.49 = (bf16[2,512,128]{2,1,0:T(8,128)(2,1)S(1)}, bf16[2,512,128]{2,1,0:T(8,128)(2,1)}, u32[]{:S(2)}, u32[]{:S(2)}) collective-permute-start(bf16[2,512,128]{2,1,0:T(8,128)(2,1)S(1)} %param.51), channel_id=1, source_target_pairs={{0,76},{4,80},{8,84},{12,88},{16,92},{20,96},{24,100},{28,104},{32... | collective-permute-start | bytes 786440 | tf_op jit(solution)/shard_map/cond/branch_19_fun/ppermute | solution.py:310
  30.5 6.4 %collective-permute-start.4 = (bf16[2,512,128]{2,1,0:T(8,128)(2,1)S(1)}, bf16[2,512,128]{2,1,0:T(8,128)(2,1)}, u32[]{:S(2)}, u32[]{:S(2)}) collective-permute-start(bf16[2,512,128]{2,1,0:T(8,128)(2,1)S(1)} %param.5), channel_id=1, source_target_pairs={{0,20},{4,24},{8,28},{12,32},{16,36},{20,40},{24,44},{28,48},{32,5... | collective-permute-start | bytes 786440 | tf_op jit(solution)/shard_map/cond/branch_5_fun/ppermute | solution.py:310
  43.0 21.1 %collective-permute-start.93 = (bf16[128,2048]{1,0:T(8,128)(2,1)}, bf16[128,2048]{1,0:T(8,128)(2,1)S(1)}, u32[]{:S(2)}, u32[]{:S(2)}) collective-permute-start(bf16[128,2048]{1,0:T(8,128)(2,1)} %attention.3), channel_id=1, source_target_pairs={{0,2},{1,3},{2,0},{3,1},{4,6},{5,7},{6,4},{7,5},{8,10},{9,11},{10,... | collective-permute-start | bytes 1572872 | tf_op jit(solution)/shard_map/ppermute | solution.py:348
  50.4 18.6 %collective-permute-start.94 = (bf16[128,2048]{1,0:T(8,128)(2,1)}, bf16[128,2048]{1,0:T(8,128)(2,1)S(1)}, u32[]{:S(2)}, u32[]{:S(2)}) collective-permute-start(bf16[128,2048]{1,0:T(8,128)(2,1)} %get-tuple-element.216), channel_id=1, source_target_pairs={{0,1},{1,2},{2,3},{3,0},{4,5},{5,6},{6,7},{7,4},{8,9},{9,10},{10,1... | collective-permute-start | bytes 1572872 | tf_op jit(solution)/shard_map/ppermute | solution.py:348
  52.4 16.7 %collective-permute-start.95 = (bf16[128,2048]{1,0:T(8,128)(2,1)}, bf16[128,2048]{1,0:T(8,128)(2,1)S(1)}, u32[]{:S(2)}, u32[]{:S(2)}) collective-permute-start(bf16[128,2048]{1,0:T(8,128)(2,1)} %get-tuple-element.217), channel_id=1, source_target_pairs={{0,3},{1,0},{2,1},{3,2},{4,7},{5,4},{6,5},{7,6},{8,11},{9,8},{10,9... | collective-permute-start | bytes 1572872 | tf_op jit(solution)/shard_map/ppermute | solution.py:348
  74.0 66.3 %all-to-all-start.2 = ((bf16[128,8,2048]{2,1,0:T(8,128)(2,1)}), bf16[128,8,2048]{2,1,0:T(8,128)(2,1)}, u32[]{:S(2)}, u32[]{:S(2)}) async-start(bf16[128,8,2048]{2,1,0:T(8,128)(2,1)} %bitcast.21), calls=%async_computation.2 | async-start | bytes 8388608 | tf_op jit(solution)/shard_map/all_to_all | solution.py:358
  140.3 57.4 %all-to-all-start = ((bf16[128,8,2048]{2,1,0:T(8,128)(2,1)}), bf16[128,8,2048]{2,1,0:T(8,128)(2,1)}, u32[]{:S(2)}, u32[]{:S(2)}) async-start(bf16[128,8,2048]{2,1,0:T(8,128)(2,1)} %bitcast.20), calls=%async_computation | async-start | bytes 8388608 | tf_op jit(solution)/shard_map/all_to_all | solution.py:358
  197.6 57.4 %all-to-all-start.3 = ((bf16[128,8,2048]{2,1,0:T(8,128)(2,1)}), bf16[128,8,2048]{2,1,0:T(8,128)(2,1)}, u32[]{:S(2)}, u32[]{:S(2)}) async-start(bf16[128,8,2048]{2,1,0:T(8,128)(2,1)} %bitcast.19), calls=%async_computation.3 | async-start | bytes 8388608 | tf_op jit(solution)/shard_map/all_to_all | solution.py:358
  255.0 57.4 %all-to-all-start.1 = ((bf16[128,8,2048]{2,1,0:T(8,128)(2,1)}), bf16[128,8,2048]{2,1,0:T(8,128)(2,1)}, u32[]{:S(2)}, u32[]{:S(2)}) async-start(bf16[128,8,2048]{2,1,0:T(8,128)(2,1)} %bitcast.18), calls=%async_computation.1 | async-start | bytes 8388608 | tf_op jit(solution)/shard_map/all_to_all | solution.py:358
where the time goes:
time: 318 us; the launch traced here: 317 us
  waiting for transfers between devices  188 us (59%)
  Pallas kernels  70.6 us (22%)
  starting transfers between devices  52.1 us (16%)
    all_to_all x4, waiting for transfers between devices, body(): lax.all_to_all(a, ALL, split_axis=0, concat_axis=0, tiled=True)  171 us
    pallas_call x2, Pallas kernels, expert(): pl.pallas_call(expert_kernel, grid=(rows // step,), in_specs=[pl.BlockSpe...  31.1 us
    all_to_all x4, starting transfers between devices, body(): lax.all_to_all(a, ALL, split_axis=0, concat_axis=0, tiled=True)  27.8 us
    ppermute x3, starting transfers between devices, back(): return lax.ppermute(block, 'ctx', [(i, i + by) for i in range(shards - by)])  19.7 us
    pallas_call x3, Pallas kernels, attention(): pl.pallas_call(functools.partial(attention_kernel, first, stride), grid_s...  18.1 us
    ppermute x3, waiting for transfers between devices, back(): return lax.ppermute(block, 'ctx', [(i, i + by) for i in range(shards - by)])  12.1 us
    pallas_call x2, Pallas kernels, combine(): pl.pallas_call(combine_kernel, grid=(count // step,), in_specs=[pl.BlockS...  8.84 us
  transfers between devices with their start and end apart: 10, of which 8 were waited for; matrix products, arithmetic and copies ran while one was open for 0% of the time, Pallas kernels for 18%

commit v1 on v0

--- a/solution.py
+++ b/solution.py
@@ -34,7 +34,7 @@
 
 
 def attention_kernel(
-    first, stride, place, wanted, q_ref, k_ref, v_ref, far0_ref, far1_ref, far2_ref, weight_ref, *refs
+    first, stride, shard, head, wanted, q_ref, k_ref, v_ref, far0_ref, far1_ref, far2_ref, weight_ref, *refs
 ):
     out_refs, (mixed_ref, w_ref, sem) = refs[:-3], refs[-3:]
     step = pl.program_id(0)
@@ -43,7 +43,7 @@
     steps = len(out_refs)
     blocks = k_ref.shape[0] // BLK
     heads = q_ref.shape[1] // HD
-    block = lax.rem(place[1] + first + stride * step, blocks)
+    block = lax.rem(head[0] + first + stride * step, blocks)
     far_refs = (far0_ref, far1_ref, far2_ref)
 
     def attend(wide):
@@ -51,7 +51,7 @@
         columns = lax.broadcasted_iota(jnp.int32, (2 * BLK, BLK), 1)
         bias = jnp.where(rows > columns + lax.rem(block, 2) * BLK, -jnp.inf, 0.0)
         bias = jnp.concatenate([bias] * heads, axis=1)
-        reach = [jnp.where(place[0] >= wanted[0, j], 0.0, -jnp.inf) for j in range(DIST)]
+        reach = [jnp.where(shard[0] >= wanted[0, j], 0.0, -jnp.inf) for j in range(DIST)]
         keys = jnp.concatenate([k_ref[:wide]] + [r[0] for r in far_refs], axis=0)
         values = jnp.concatenate([v_ref[:wide]] + [r[1] for r in far_refs], axis=0)
         query = jnp.concatenate([q_ref[:, n * HD : (n + 1) * HD] for n in range(heads)], axis=0)
@@ -84,24 +84,24 @@
             ).astype(BF16)
 
 
-def attention(place, wanted, queries, keys, values, far, out_weight, first, stride, steps):
+def attention(shard, head, wanted, queries, keys, values, far, out_weight, first, stride, steps):
     length, wide = queries.shape
     width = out_weight.shape[1]
-    at = lambda i, place: lax.rem(place[1] + first + stride * i, length // BLK)
+    at = lambda i, head: lax.rem(head[0] + first + stride * i, length // BLK)
     whole = lambda shape: pl.BlockSpec(
-        shape, lambda i, p, w: (0,) * len(shape), pipeline_mode=pl.Buffered(1)
+        shape, lambda i, s, h, w: (0,) * len(shape), pipeline_mode=pl.Buffered(1)
     )
     return pl.pallas_call(
         functools.partial(attention_kernel, first, stride),
         grid_spec=pltpu.PrefetchScalarGridSpec(
-            num_scalar_prefetch=2,
+            num_scalar_prefetch=3,
             grid=(steps,),
             in_specs=[
-                pl.BlockSpec((BLK, wide), lambda i, p, w: (at(i, p), 0)),
+                pl.BlockSpec((BLK, wide), lambda i, s, h, w: (at(i, h), 0)),
                 whole(keys.shape),
                 whole(values.shape),
             ]
-            + [pl.BlockSpec((2, BLK, HD), lambda i, p, w: (0, at(i, p), 0))] * DIST
+            + [pl.BlockSpec((2, BLK, HD), lambda i, s, h, w: (0, at(i, h), 0))] * DIST
             + [pl.BlockSpec(memory_space=pl.ANY)],
             out_specs=(whole((BLK, width)),) * steps,
             scratch_shapes=[
@@ -113,7 +113,7 @@
         out_shape=(jax.ShapeDtypeStruct((BLK, width), BF16),) * steps,
         compiler_params=params(),
         name="attention",
-    )(place, wanted, queries, keys, values, *far, out_weight)
+    )(shard, head, wanted, queries, keys, values, *far, out_weight)
 
 
 def tables_kernel(routes_ref, weights_ref, *refs):
@@ -337,11 +337,11 @@
     send, table = tables(routes, route_weights, devices)
     group = lax.axis_size("head")
 
-    place = jnp.stack([me, head])
+    shard, place = me.reshape(1), head.reshape(1)
 
     def project(place, first, stride, steps):
         return attention(
-            place, distances, queries, keys, values, far, out_weight, first, stride, steps
+            shard, place, distances, queries, keys, values, far, out_weight, first, stride, steps
         )
 
     def hand(block, by):

time: 318 us -> 320 us (level)
  starting transfers between devices: 52.1 us -> 56.8 us
  transfers between devices with their start and end apart: 10 -> 10, of which waited for: 8 -> 9; matrix products, arithmetic and copies ran while one was open for 0% -> 0% of each run, Pallas kernels for 18% -> 17%
where the time goes in v1:
time: 320 us
  waiting for transfers between devices  187 us (58%)
  Pallas kernels  70.5 us (22%)
  starting transfers between devices  56.8 us (18%)
    all_to_all x4, waiting for transfers between devices, body(): lax.all_to_all(a, ALL, split_axis=0, concat_axis=0, tiled=True)  171 us
    pallas_call x2, Pallas kernels, expert(): pl.pallas_call(expert_kernel, grid=(rows // step,), in_specs=[pl.BlockSpe...  31.1 us
    all_to_all x4, starting transfers between devices, body(): lax.all_to_all(a, ALL, split_axis=0, concat_axis=0, tiled=True)  30.5 us
    ppermute x3, starting transfers between devices, back(): return lax.ppermute(block, 'ctx', [(i, i + by) for i in range(shards - by)])  19.7 us
    pallas_call x3, Pallas kernels, attention(): pl.pallas_call(functools.partial(attention_kernel, first, stride), grid_s...  18 us
    ppermute x3, waiting for transfers between devices, back(): return lax.ppermute(block, 'ctx', [(i, i + by) for i in range(shards - by)])  9.7 us
    pallas_call x2, Pallas kernels, combine(): pl.pallas_call(combine_kernel, grid=(count // step,), in_specs=[pl.BlockS...  8.84 us
    ppermute x3, waiting for transfers between devices, hand(): lax.ppermute(block, 'head', [(i, (i + by) % group) for i in range(group)])  6.58 us
  transfers between devices with their start and end apart: 10, of which 9 were waited for; matrix products, arithmetic and copies ran while one was open for 0% of the time, Pallas kernels for 17%

profile of v1, /device:TPU:1, one launch (start us, length us, event | category | flops | bytes accessed | tf_op | source)
XLA Modules:
  0.0 319.8 jit_solution(82752540144117662)
XLA Ops:
  0.6 1.4 fusion
  4.9 7.9 %conditional.5 = (bf16[2,512,128]{2,1,0:T(8,128)(2,1)}) conditional(s32[]{:T(128)} %bitcast.6, bf16[2,512,128]{2,1,0:T(8,128)(2,1)S(1)} %pad_maximum_fusion, bf16[2,512,128]{2,1,0:T(8,128)(2,1)S(1)} %pad_maximum_fusion, bf16[2,512,128]{2,1,0:T(8,128)(2,1)S(1)} %pad_maximum_fusion, ...), branch_computations={%region_64.0_spmd, %region_65.0_spmd, %region_66.0_spmd, %region_6... | conditional | bytes 1048624 | solution.py:312
  4.9 4.5 %collective-permute-start.62 = (bf16[2,512,128]{2,1,0:T(8,128)(2,1)S(1)}, bf16[2,512,128]{2,1,0:T(8,128)(2,1)}, u32[]{:S(2)}, u32[]{:S(2)}) collective-permute-start(bf16[2,512,128]{2,1,0:T(8,128)(2,1)S(1)} %param.65), channel_id=1, source_target_pairs={{0,4},{4,8},{8,12},{12,16},{16,20},{20,24},{24,28},{28,32},{32,36}... | collective-permute-start | bytes 786440 | tf_op jit(solution)/shard_map/cond/branch_1_fun/ppermute | solution.py:310
  9.4 3.3 %collective-permute-done.62 = bf16[2,512,128]{2,1,0:T(8,128)(2,1)} collective-permute-done((bf16[2,512,128]{2,1,0:T(8,128)(2,1)S(1)}, bf16[2,512,128]{2,1,0:T(8,128)(2,1)}, u32[]{:S(2)}, u32[]{:S(2)}) %collective-permute-start.62) | collective-permute-done | bytes 262176 | tf_op jit(solution)/shard_map/cond/branch_1_fun/ppermute | solution.py:310
  12.7 9.2 %conditional.4 = (bf16[2,512,128]{2,1,0:T(8,128)(2,1)}) conditional(s32[]{:T(128)} %bitcast.5, bf16[2,512,128]{2,1,0:T(8,128)(2,1)S(1)} %pad_maximum_fusion, bf16[2,512,128]{2,1,0:T(8,128)(2,1)S(1)} %pad_maximum_fusion, bf16[2,512,128]{2,1,0:T(8,128)(2,1)S(1)} %pad_maximum_fusion, ...), branch_computations={%region_32.0_spmd, %region_33.0_spmd, %region_34.0_spmd, %region_3... | conditional | bytes 1048624 | solution.py:312
  12.7 5.4 %collective-permute-start.36 = (bf16[2,512,128]{2,1,0:T(8,128)(2,1)S(1)}, bf16[2,512,128]{2,1,0:T(8,128)(2,1)}, u32[]{:S(2)}, u32[]{:S(2)}) collective-permute-start(bf16[2,512,128]{2,1,0:T(8,128)(2,1)S(1)} %param.38), channel_id=1, source_target_pairs={{0,24},{4,28},{8,32},{12,36},{16,40},{20,44},{24,48},{28,52},{32,5... | collective-permute-start | bytes 786440 | tf_op jit(solution)/shard_map/cond/branch_6_fun/ppermute | solution.py:310
  18.2 3.7 %collective-permute-done.36 = bf16[2,512,128]{2,1,0:T(8,128)(2,1)} collective-permute-done((bf16[2,512,128]{2,1,0:T(8,128)(2,1)S(1)}, bf16[2,512,128]{2,1,0:T(8,128)(2,1)}, u32[]{:S(2)}, u32[]{:S(2)}) %collective-permute-start.36) | collective-permute-done | bytes 262176 | tf_op jit(solution)/shard_map/cond/branch_6_fun/ppermute | solution.py:310
  21.9 12.5 %conditional.3 = (bf16[2,512,128]{2,1,0:T(8,128)(2,1)}) conditional(s32[]{:T(128)} %bitcast.2, bf16[2,512,128]{2,1,0:T(8,128)(2,1)S(1)} %pad_maximum_fusion, bf16[2,512,128]{2,1,0:T(8,128)(2,1)S(1)} %pad_maximum_fusion, bf16[2,512,128]{2,1,0:T(8,128)(2,1)S(1)} %pad_maximum_fusion, ...), branch_computations={%region_0.0_spmd, %region_1.0_spmd, %region_2.0_spmd, %region_3.0_... | conditional | bytes 1048624 | solution.py:312
  21.9 9.8 %collective-permute-start.14 = (bf16[2,512,128]{2,1,0:T(8,128)(2,1)S(1)}, bf16[2,512,128]{2,1,0:T(8,128)(2,1)}, u32[]{:S(2)}, u32[]{:S(2)}) collective-permute-start(bf16[2,512,128]{2,1,0:T(8,128)(2,1)S(1)} %param.15), channel_id=1, source_target_pairs={{0,60},{4,64},{8,68},{12,72},{16,76},{20,80},{24,84},{28,88},{32,9... | collective-permute-start | bytes 786440 | tf_op jit(solution)/shard_map/cond/branch_15_fun/ppermute | solution.py:310
  31.7 2.7 collective-permute-done.14
  34.4 5.5 %attention.3 = bf16[128,2048]{1,0:T(8,128)(2,1)} custom-call(s32[1]{0:T(128)} %bitcast.shard, s32[1]{0:T(128)} %bitcast.1.head, s32[1,3]{1,0:T(1,128)} %wanted.5, bf16[512,1024]{1,0:T(8,128)(2,1)} %q_ref.5, bf16[512,128]{1,0:T(8,128)(2,1)} %k_ref.5, bf16[512,128]{1,0:T(8,128)(2,1)} %v_ref.5, bf16[2,512,128]{2,1,0:T(8,128)(2,1)} %get-tuple-element.228.far0_ref, ...), custom_call_target="tpu_custom_call" | custom-call | tf_op jit(solution)/shard_map/attention/pallas_call | solution.py:94
  39.9 3.8 %collective-permute-start.93 = (bf16[128,2048]{1,0:T(8,128)(2,1)}, bf16[128,2048]{1,0:T(8,128)(2,1)S(1)}, u32[]{:S(2)}, u32[]{:S(2)}) collective-permute-start(bf16[128,2048]{1,0:T(8,128)(2,1)} %attention.3), channel_id=1, source_target_pairs={{0,2},{1,3},{2,0},{3,1},{4,6},{5,7},{6,4},{7,5},{8,10},{9,11},{10,... | collective-permute-start | bytes 1572872 | tf_op jit(solution)/shard_map/ppermute | solution.py:348
  43.7 7.1 %attention.4 = (bf16[128,2048]{1,0:T(8,128)(2,1)}, bf16[128,2048]{1,0:T(8,128)(2,1)}) custom-call(s32[1]{0:T(128)} %bitcast.shard, s32[1]{0:T(128)} %bitcast.1.head, s32[1,3]{1,0:T(1,128)} %wanted.5, bf16[512,1024]{1,0:T(8,128)(2,1)} %q_ref.5, bf16[512,128]{1,0:T(8,128)(2,1)} %k_ref.5, bf16[512,128]{1,0:T(8,128)(2,1)} %v_ref.5, ...), custom_call_target="tpu_custom_call" | custom-call | tf_op jit(solution)/shard_map/attention/pallas_call | solution.py:94
  50.8 2.5 collective-permute-start.94
  53.5 5.5 %attention.5.own_ref = bf16[128,2048]{1,0:T(8,128)(2,1)} custom-call(s32[1]{0:T(128)} %bitcast.shard, s32[1]{0:T(128)} %bitcast.1.head, s32[1,3]{1,0:T(1,128)} %wanted.5, bf16[512,1024]{1,0:T(8,128)(2,1)} %q_ref.5, bf16[512,128]{1,0:T(8,128)(2,1)} %k_ref.5, bf16[512,128]{1,0:T(8,128)(2,1)} %v_ref.5, bf16[2,512,128]{2,1,0:T(8,128)(2,1)} %get-tuple-element.228.far0_ref, ...), custom_call_target="tpu_custom_call" | custom-call | tf_op jit(solution)/shard_map/attention/pallas_call | solution.py:94
  59.0 3.8 %tables.1 = (bf16[1024,128]{1,0:T(8,128)(2,1)}, bf16[1024,128]{1,0:T(8,128)(2,1)}, bf16[1024,256]{1,0:T(8,128)(2,1)}, bf16[1024,256]{1,0:T(8,128)(2,1)}) custom-call(s32[8,128]{1,0:T(8,128)} %bitcast.25, f32[8,128]{1,0:T(8,128)} %bitcast.26), custom_call_target="tpu_custom_call" | custom-call | tf_op jit(solution)/shard_map/tables/pallas_call | solution.py:161
  62.8 3.1 collective-permute-done.94.r2_ref
  65.8 3.5 %collective-permute-done.95.r3_ref = bf16[128,2048]{1,0:T(8,128)(2,1)S(1)} collective-permute-done((bf16[128,2048]{1,0:T(8,128)(2,1)}, bf16[128,2048]{1,0:T(8,128)(2,1)S(1)}, u32[]{:S(2)}, u32[]{:S(2)}) %collective-permute-start.95) | collective-permute-done | bytes 524320 | tf_op jit(solution)/shard_map/ppermute | solution.py:348
  69.3 4.9 %norm_dispatch.1 = (bf16[128,2048]{1,0:T(8,128)(2,1)}, bf16[128,2048]{1,0:T(8,128)(2,1)}, bf16[1024,2048]{1,0:T(8,128)(2,1)}) custom-call(bf16[128,2048]{1,0:T(8,128)(2,1)} %attention.5.own_ref, bf16[128,2048]{1,0:T(8,128)(2,1)S(1)} %collective-permute-done.93.r1_ref, bf16[128,2048]{1,0:T(8,128)(2,1)S(1)} %collective-permute-done.94.r2_ref, ...), custom_call_target="tpu_custom_call" | custom-call | tf_op jit(solution)/shard_map/norm_dispatch/pallas_call | solution.py:193
  74.2 16.2 %all-to-all-start.2 = ((bf16[128,8,2048]{2,1,0:T(8,128)(2,1)}), bf16[128,8,2048]{2,1,0:T(8,128)(2,1)}, u32[]{:S(2)}, u32[]{:S(2)}) async-start(bf16[128,8,2048]{2,1,0:T(8,128)(2,1)} %bitcast.21), calls=%async_computation.2 | async-start | bytes 8388608 | tf_op jit(solution)/shard_map/all_to_all | solution.py:358
  90.4 3.9 %dispatch.1 = bf16[1024,2048]{1,0:T(8,128)(2,1)} custom-call(bf16[1024,128]{1,0:T(8,128)(2,1)} %get-tuple-element.221.send_ref, bf16[128,2048]{1,0:T(8,128)(2,1)} %get-tuple-element.222.normed_ref), custom_call_target="tpu_custom_call" | custom-call | tf_op jit(solution)/shard_map/dispatch/pallas_call | solution.py:222
  94.4 48.9 %all-to-all-done.2 = bf16[128,8,2048]{2,1,0:T(8,128)(2,1)} async-done(((bf16[128,8,2048]{2,1,0:T(8,128)(2,1)}), bf16[128,8,2048]{2,1,0:T(8,128)(2,1)}, u32[]{:S(2)}, u32[]{:S(2)}) %all-to-all-start.2) | async-done | bytes 4194336 | tf_op jit(solution)/shard_map/all_to_all | solution.py:358
  143.3 4.8 %all-to-all-start = ((bf16[128,8,2048]{2,1,0:T(8,128)(2,1)}), bf16[128,8,2048]{2,1,0:T(8,128)(2,1)}, u32[]{:S(2)}, u32[]{:S(2)}) async-start(bf16[128,8,2048]{2,1,0:T(8,128)(2,1)} %bitcast.20), calls=%async_computation | async-start | bytes 8388608 | tf_op jit(solution)/shard_map/all_to_all | solution.py:358
  148.1 15.6 %expert.3 = bf16[1024,2048]{1,0:T(8,128)(2,1)} custom-call(bf16[1024,2048]{1,0:T(8,128)(2,1)} %bitcast.15.x_ref, bf16[1,2048,1536]{2,1,0:T(8,128)(2,1)} %gate_up_ref.3, bf16[1,768,2048]{2,1,0:T(8,128)(2,1)} %down_ref.3), custom_call_target="tpu_custom_call" | custom-call | tf_op jit(solution)/shard_map/expert/pallas_call | solution.py:249
  163.6 37.0 %all-to-all-done = bf16[128,8,2048]{2,1,0:T(8,128)(2,1)} async-done(((bf16[128,8,2048]{2,1,0:T(8,128)(2,1)}), bf16[128,8,2048]{2,1,0:T(8,128)(2,1)}, u32[]{:S(2)}, u32[]{:S(2)}) %all-to-all-start) | async-done | bytes 4194336 | tf_op jit(solution)/shard_map/all_to_all | solution.py:358
  200.6 4.8 %all-to-all-start.3 = ((bf16[128,8,2048]{2,1,0:T(8,128)(2,1)}), bf16[128,8,2048]{2,1,0:T(8,128)(2,1)}, u32[]{:S(2)}, u32[]{:S(2)}) async-start(bf16[128,8,2048]{2,1,0:T(8,128)(2,1)} %bitcast.19), calls=%async_computation.3 | async-start | bytes 8388608 | tf_op jit(solution)/shard_map/all_to_all | solution.py:358
  205.4 15.5 %expert.2 = bf16[1024,2048]{1,0:T(8,128)(2,1)} custom-call(bf16[1024,2048]{1,0:T(8,128)(2,1)} %bitcast.11.x_ref, bf16[1,2048,1536]{2,1,0:T(8,128)(2,1)} %gate_up_ref.3, bf16[1,768,2048]{2,1,0:T(8,128)(2,1)} %down_ref.3), custom_call_target="tpu_custom_call" | custom-call | tf_op jit(solution)/shard_map/expert/pallas_call | solution.py:249
  220.9 37.1 %all-to-all-done.3 = bf16[128,8,2048]{2,1,0:T(8,128)(2,1)} async-done(((bf16[128,8,2048]{2,1,0:T(8,128)(2,1)}), bf16[128,8,2048]{2,1,0:T(8,128)(2,1)}, u32[]{:S(2)}, u32[]{:S(2)}) %all-to-all-start.3) | async-done | bytes 4194336 | tf_op jit(solution)/shard_map/all_to_all | solution.py:358
  258.0 4.8 %all-to-all-start.1 = ((bf16[128,8,2048]{2,1,0:T(8,128)(2,1)}), bf16[128,8,2048]{2,1,0:T(8,128)(2,1)}, u32[]{:S(2)}, u32[]{:S(2)}) async-start(bf16[128,8,2048]{2,1,0:T(8,128)(2,1)} %bitcast.18), calls=%async_computation.1 | async-start | bytes 8388608 | tf_op jit(solution)/shard_map/all_to_all | solution.py:358
  262.8 4.4 %combine.2.refs_0_ = f32[128,2048]{1,0:T(8,128)} custom-call(bf16[1024,256]{1,0:T(8,128)(2,1)} %get-tuple-element.223.table_ref, bf16[1024,2048]{1,0:T(8,128)(2,1)} %bitcast.17.rows_ref), custom_call_target="tpu_custom_call" | custom-call | tf_op jit(solution)/shard_map/combine/pallas_call | solution.py:290
  267.1 48.2 %all-to-all-done.1 = bf16[128,8,2048]{2,1,0:T(8,128)(2,1)} async-done(((bf16[128,8,2048]{2,1,0:T(8,128)(2,1)}), bf16[128,8,2048]{2,1,0:T(8,128)(2,1)}, u32[]{:S(2)}, u32[]{:S(2)}) %all-to-all-start.1) | async-done | bytes 4194336 | tf_op jit(solution)/shard_map/all_to_all | solution.py:358
  315.3 4.5 %combine.3 = bf16[128,2048]{1,0:T(8,128)(2,1)} custom-call(bf16[1024,256]{1,0:T(8,128)(2,1)} %get-tuple-element.220.table_ref, bf16[1024,2048]{1,0:T(8,128)(2,1)} %bitcast.13.rows_ref, f32[128,2048]{1,0:T(8,128)} %combine.2.refs_0_), custom_call_target="tpu_custom_call" | custom-call | tf_op jit(solution)/shard_map/combine/pallas_call | solution.py:290
  (3 shorter events, 1.3 us)
Async XLA Ops:
  4.9 7.8 %collective-permute-start.62 = (bf16[2,512,128]{2,1,0:T(8,128)(2,1)S(1)}, bf16[2,512,128]{2,1,0:T(8,128)(2,1)}, u32[]{:S(2)}, u32[]{:S(2)}) collective-permute-start(bf16[2,512,128]{2,1,0:T(8,128)(2,1)S(1)} %param.65), channel_id=1, source_target_pairs={{0,4},{4,8},{8,12},{12,16},{16,20},{20,24},{24,28},{28,32},{32,36}... | collective-permute-start | bytes 786440 | tf_op jit(solution)/shard_map/cond/branch_1_fun/ppermute | solution.py:310
  12.7 9.2 %collective-permute-start.36 = (bf16[2,512,128]{2,1,0:T(8,128)(2,1)S(1)}, bf16[2,512,128]{2,1,0:T(8,128)(2,1)}, u32[]{:S(2)}, u32[]{:S(2)}) collective-permute-start(bf16[2,512,128]{2,1,0:T(8,128)(2,1)S(1)} %param.38), channel_id=1, source_target_pairs={{0,24},{4,28},{8,32},{12,36},{16,40},{20,44},{24,48},{28,52},{32,5... | collective-permute-start | bytes 786440 | tf_op jit(solution)/shard_map/cond/branch_6_fun/ppermute | solution.py:310
  21.9 12.5 %collective-permute-start.14 = (bf16[2,512,128]{2,1,0:T(8,128)(2,1)S(1)}, bf16[2,512,128]{2,1,0:T(8,128)(2,1)}, u32[]{:S(2)}, u32[]{:S(2)}) collective-permute-start(bf16[2,512,128]{2,1,0:T(8,128)(2,1)S(1)} %param.15), channel_id=1, source_target_pairs={{0,60},{4,64},{8,68},{12,72},{16,76},{20,80},{24,84},{28,88},{32,9... | collective-permute-start | bytes 786440 | tf_op jit(solution)/shard_map/cond/branch_15_fun/ppermute | solution.py:310
  39.9 22.9 %collective-permute-start.93 = (bf16[128,2048]{1,0:T(8,128)(2,1)}, bf16[128,2048]{1,0:T(8,128)(2,1)S(1)}, u32[]{:S(2)}, u32[]{:S(2)}) collective-permute-start(bf16[128,2048]{1,0:T(8,128)(2,1)} %attention.3), channel_id=1, source_target_pairs={{0,2},{1,3},{2,0},{3,1},{4,6},{5,7},{6,4},{7,5},{8,10},{9,11},{10,... | collective-permute-start | bytes 1572872 | tf_op jit(solution)/shard_map/ppermute | solution.py:348
  50.8 15.1 %collective-permute-start.94 = (bf16[128,2048]{1,0:T(8,128)(2,1)}, bf16[128,2048]{1,0:T(8,128)(2,1)S(1)}, u32[]{:S(2)}, u32[]{:S(2)}) collective-permute-start(bf16[128,2048]{1,0:T(8,128)(2,1)} %get-tuple-element.216), channel_id=1, source_target_pairs={{0,1},{1,2},{2,3},{3,0},{4,5},{5,6},{6,7},{7,4},{8,9},{9,10},{10,1... | collective-permute-start | bytes 1572872 | tf_op jit(solution)/shard_map/ppermute | solution.py:348
  53.2 16.1 %collective-permute-start.95 = (bf16[128,2048]{1,0:T(8,128)(2,1)}, bf16[128,2048]{1,0:T(8,128)(2,1)S(1)}, u32[]{:S(2)}, u32[]{:S(2)}) collective-permute-start(bf16[128,2048]{1,0:T(8,128)(2,1)} %get-tuple-element.217), channel_id=1, source_target_pairs={{0,3},{1,0},{2,1},{3,2},{4,7},{5,4},{6,5},{7,6},{8,11},{9,8},{10,9... | collective-permute-start | bytes 1572872 | tf_op jit(solution)/shard_map/ppermute | solution.py:348
  74.2 69.0 %all-to-all-start.2 = ((bf16[128,8,2048]{2,1,0:T(8,128)(2,1)}), bf16[128,8,2048]{2,1,0:T(8,128)(2,1)}, u32[]{:S(2)}, u32[]{:S(2)}) async-start(bf16[128,8,2048]{2,1,0:T(8,128)(2,1)} %bitcast.21), calls=%async_computation.2 | async-start | bytes 8388608 | tf_op jit(solution)/shard_map/all_to_all | solution.py:358
  143.3 57.4 %all-to-all-start = ((bf16[128,8,2048]{2,1,0:T(8,128)(2,1)}), bf16[128,8,2048]{2,1,0:T(8,128)(2,1)}, u32[]{:S(2)}, u32[]{:S(2)}) async-start(bf16[128,8,2048]{2,1,0:T(8,128)(2,1)} %bitcast.20), calls=%async_computation | async-start | bytes 8388608 | tf_op jit(solution)/shard_map/all_to_all | solution.py:358
  200.6 57.4 %all-to-all-start.3 = ((bf16[128,8,2048]{2,1,0:T(8,128)(2,1)}), bf16[128,8,2048]{2,1,0:T(8,128)(2,1)}, u32[]{:S(2)}, u32[]{:S(2)}) async-start(bf16[128,8,2048]{2,1,0:T(8,128)(2,1)} %bitcast.19), calls=%async_computation.3 | async-start | bytes 8388608 | tf_op jit(solution)/shard_map/all_to_all | solution.py:358
  258.0 57.4 %all-to-all-start.1 = ((bf16[128,8,2048]{2,1,0:T(8,128)(2,1)}), bf16[128,8,2048]{2,1,0:T(8,128)(2,1)}, u32[]{:S(2)}, u32[]{:S(2)}) async-start(bf16[128,8,2048]{2,1,0:T(8,128)(2,1)} %bitcast.18), calls=%async_computation.1 | async-start | bytes 8388608 | tf_op jit(solution)/shard_map/all_to_all | solution.py:358
